TPU v7x, 512 devices: a whole 4x4x16 slice. The times are simulated.
512 devices in a mesh: gz: 16 (over z), gy: 32 (over x, y, core).
Axes of the slice: x: 4, y: 4, z: 16, core: 2. Of those that a mesh axis runs over, the one named last changes fastest.
Arguments:
- tracer: float32 [512, 1024, 128], P('gz', 'gy'), may hold values from 0.1 to 10
- y_speed: float32 [512, 1024, 128], P('gz', 'gy'), may hold values from -0.4 to 0.4
- z_speed: float32 [512, 1024, 128], P('gz', 'gy'), may hold values from -0.4 to 0.4
- kappa: float32 [512, 1024, 128], P('gz', 'gy'), may hold values from 0.5 to 8
Outputs:
- updated: float32 [512, 1024, 128], P('gz', 'gy')
All inputs are finite; a program needn't handle non-finite values.
Results may differ from a plain program's by a relative error of at most 0.0003.
Values sent between devices are 32-bit elements; how exact they have to be, the bound alone decides.
A program may use at most 64 MiB of HBM per device.

v0:
```python
import jax
import jax.numpy as jnp
from jax import lax
from jax.sharding import PartitionSpec as P

NSUB = 4
rate_const = 500.0


def padded_2(x, sides, width):
    for axis, dim in sides:
        peers, length = (lax.axis_size(axis), x.shape[dim])
        up = [(i, (i + 1) % peers) for i in range(peers - 1)]
        down = [(j, i) for i, j in up]
        last = lax.slice_in_dim(x, length - width, length, axis=dim)
        leading = lax.slice_in_dim(x, 0, width, axis=dim)
        before = lax.ppermute(last, axis, up)
        after = lax.ppermute(leading, axis, down)
        x = jnp.concatenate([before, x, after], axis=dim)
    return x


def from_behind(x, axis, by):
    peers = lax.axis_size(axis)
    pairs = [(i, i + by) for i in range(peers) if 0 <= i + by < peers]
    return lax.ppermute(x, axis, pairs)


def advect_once(tracer, y_speed, z_speed):
    face_y = 0.5 * (y_speed[:, 1:] + y_speed[:, :-1])
    flux_y = jnp.maximum(face_y, 0.0) * tracer[:, :-1] + jnp.minimum(face_y, 0.0) * tracer[:, 1:]
    diff_y = flux_y[:, 1:] - flux_y[:, :-1]
    face_z = 0.5 * (z_speed[1:] + z_speed[:-1])
    flux_z = jnp.maximum(face_z, 0.0) * tracer[:-1] + jnp.minimum(face_z, 0.0) * tracer[1:]
    diff_z = flux_z[1:] - flux_z[:-1]
    return tracer[1:-1, 1:-1] - diff_y[1:-1] - diff_z[:, 1:-1]


def move_down(values, offset, axis, fill):
    count = values.shape[axis]
    kept = lax.slice_in_dim(values, 0, count - offset, axis=axis)
    padding = jnp.full_like(lax.slice_in_dim(values, 0, offset, axis=axis), fill)
    return jnp.concatenate([padding, kept], axis=axis)


def move_up(values, offset, axis, fill):
    count = values.shape[axis]
    kept = lax.slice_in_dim(values, offset, count, axis=axis)
    padding = jnp.full_like(lax.slice_in_dim(values, 0, offset, axis=axis), fill)
    return jnp.concatenate([kept, padding], axis=axis)


def reduce_lines(sub_diag, main_diag, sup_diag, rights, axis):
    count = main_diag.shape[axis]
    offset = 1
    while offset < count:
        factor_low = -sub_diag / move_down(main_diag, offset, axis, 1.0)
        factor_high = -sup_diag / move_up(main_diag, offset, axis, 1.0)
        new_main = (
            main_diag
            + factor_low * move_down(sup_diag, offset, axis, 0.0)
            + factor_high * move_up(sub_diag, offset, axis, 0.0)
        )
        new_sub = factor_low * move_down(sub_diag, offset, axis, 0.0)
        new_sup = factor_high * move_up(sup_diag, offset, axis, 0.0)
        rights = tuple(
            (
                right
                + factor_low * move_down(right, offset, axis, 0.0)
                + factor_high * move_up(right, offset, axis, 0.0)
                for right in rights
            )
        )
        sub_diag, main_diag, sup_diag = (new_sub, new_main, new_sup)
        offset = offset * 2
    return tuple((right / main_diag for right in rights))


def solve_rows(items):
    tracer_part, kappa_part = items
    count = kappa_part.shape[1]
    inner = rate_const * 0.5 * (kappa_part[:, 1:] + kappa_part[:, :-1])
    lower = jnp.concatenate([rate_const * kappa_part[:, :1], inner], axis=1)
    upper = jnp.concatenate([inner, rate_const * kappa_part[:, count - 1 :]], axis=1)
    main_diag = 1.0 + lower + upper
    zero_row = jnp.zeros_like(kappa_part[:, :1])
    sub_diag = jnp.concatenate([zero_row, -inner], axis=1)
    sup_diag = jnp.concatenate([-inner, zero_row], axis=1)
    solved = reduce_lines(sub_diag, main_diag, sup_diag, (tracer_part,), 1)[0]
    return lax.all_to_all(solved, "gy", split_axis=1, concat_axis=0, tiled=True)


def local(tracer, y_speed, z_speed, kappa):
    depth_z, depth_y, band = tracer.shape
    z_index = lax.axis_index("gz")
    z_count = lax.axis_size("gz")
    fields = jnp.stack([y_speed, z_speed, kappa])
    width = 1
    padded = padded_2(fields, (("gz", 1), ("gy", 2)), 1)
    state = tracer
    for step in range(NSUB):
        rimmed = padded_2(state, (("gz", 0), ("gy", 1)), 1)
        state = advect_once(rimmed, padded[0], padded[1])
    kappa_below = padded[2, width - 1 : width, width : width + depth_y]
    kappa_above = padded[2, width + depth_z : width + depth_z + 1, width : width + depth_y]
    lines = solve_rows(
        (
            lax.all_to_all(state, "gy", split_axis=0, concat_axis=1, tiled=True),
            lax.all_to_all(kappa, "gy", split_axis=0, concat_axis=1, tiled=True),
        )
    )
    inner = rate_const * 0.5 * (kappa[1:] + kappa[:-1])
    low_edge = jnp.where(
        z_index == 0, rate_const * kappa[:1], rate_const * 0.5 * (kappa[:1] + kappa_below)
    )
    high_edge = jnp.where(
        z_index == z_count - 1,
        rate_const * kappa[depth_z - 1 :],
        rate_const * 0.5 * (kappa[depth_z - 1 :] + kappa_above),
    )
    lower = jnp.concatenate([low_edge, inner], axis=0)
    upper = jnp.concatenate([inner, high_edge], axis=0)
    main_diag = 1.0 + lower + upper
    inner_count = depth_z - 1
    zero_row = jnp.zeros_like(kappa[:1])
    sub_local = jnp.concatenate([zero_row, -lower[1:inner_count]], axis=0)
    sup_local = jnp.concatenate([-upper[: inner_count - 1], zero_row], axis=0)
    zero_rows = jnp.zeros_like(kappa[: inner_count - 1])
    first_right = jnp.concatenate([lower[:1], zero_rows], axis=0)
    last_right = jnp.concatenate([zero_rows, upper[inner_count - 1 : inner_count]], axis=0)
    base, toward_low, toward_high = reduce_lines(
        sub_local,
        main_diag[:inner_count],
        sup_local,
        (lines[:inner_count], first_right, last_right),
        0,
    )
    following = from_behind(jnp.stack([base[0], toward_low[0], toward_high[0]]), "gz", -1)
    sep_low = lower[depth_z - 1]
    sep_high = upper[depth_z - 1]
    sub_red = jnp.where(z_index == 0, 0.0, -sep_low * toward_low[inner_count - 1])
    diag_red = (
        main_diag[depth_z - 1] - sep_low * toward_high[inner_count - 1] - sep_high * following[1]
    )
    sup_red = -sep_high * following[2]
    rhs_red = lines[depth_z - 1] + sep_low * base[inner_count - 1] + sep_high * following[0]
    equations = jnp.stack([sub_red, diag_red, sup_red, rhs_red])
    collected = lax.all_gather(equations[None], "gz", axis=0, tiled=True)
    values = reduce_lines(collected[:, 0], collected[:, 1], collected[:, 2], (collected[:, 3],), 0)[
        0
    ]
    sep_here = lax.dynamic_index_in_dim(values, z_index, axis=0, keepdims=False)
    previous = lax.dynamic_index_in_dim(values, jnp.maximum(z_index - 1, 0), axis=0, keepdims=False)
    sep_prev = jnp.where(z_index > 0, previous, 0.0)
    interior = base + sep_prev[None] * toward_low + sep_here[None] * toward_high
    return jnp.concatenate([interior, sep_here[None]], axis=0)


def solution(mesh):
    return jax.shard_map(
        local,
        mesh=mesh,
        in_specs=(
            P("gz", "gy", None),
            P("gz", "gy", None),
            P("gz", "gy", None),
            P("gz", "gy", None),
        ),
        out_specs=P("gz", "gy", None),
        check_vma=False,
    )
```

profile of v0, /device:TPU:2, one launch (start us, length us, event | category | flops | bytes accessed | tf_op | source)
XLA Modules:
  0.0 254.8 jit_solution(3350201011597019658)
XLA Ops:
  6.5 0.9 fusion.100
  7.4 3.8 %collective-permute-start.4 = (f32[1,32,128]{2,1,0:T(8,128)S(1)}, f32[1,32,128]{2,1,0:T(8,128)S(1)}, u32[]{:S(2)}, u32[]{:S(2)}) collective-permute-start(f32[1,32,128]{2,1,0:T(8,128)S(1)} %get-tuple-element.204), channel_id=1, source_target_pairs={{0,32},{32,64},{64,96},{96,128},{128,160},{160,192},{192,224},{224... | collective-permute-start | bytes 49160 | tf_op jit(solution)/shard_map/ppermute | solution.py:17
  12.0 3.8 %collective-permute-start = (f32[3,1,32,128]{3,2,1,0:T(8,128)S(1)}, f32[3,1,32,128]{3,2,1,0:T(8,128)S(1)}, u32[]{:S(2)}, u32[]{:S(2)}) collective-permute-start(f32[3,1,32,128]{3,2,1,0:T(8,128)S(1)} %get-tuple-element.65), channel_id=1, source_target_pairs={{0,32},{32,64},{64,96},{96,128},{128,160},{160,192},{192,224},{224... | collective-permute-start | bytes 147464 | tf_op jit(solution)/shard_map/ppermute | solution.py:17
  15.9 1.3 collective-permute-start.1
  17.2 1.3 collective-permute-start.5
  18.5 4.9 %collective-permute-done.5 = f32[1,32,128]{2,1,0:T(8,128)S(1)} collective-permute-done((f32[1,32,128]{2,1,0:T(8,128)S(1)}, f32[1,32,128]{2,1,0:T(8,128)S(1)}, u32[]{:S(2)}, u32[]{:S(2)}) %collective-permute-start.5) | collective-permute-done | bytes 16416 | tf_op jit(solution)/shard_map/ppermute | solution.py:18
  23.5 1.9 collective-permute-start.6
  25.4 5.8 %collective-permute-start.7 = (f32[34,1,128]{2,1,0:T(1,128)S(1)}, f32[34,1,128]{2,1,0:T(1,128)S(1)}, u32[]{:S(2)}, u32[]{:S(2)}) collective-permute-start(f32[34,1,128]{2,1,0:T(1,128)S(1)} %get-tuple-element.114), channel_id=1, source_target_pairs={{1,0},{2,1},{3,2},{4,3},{5,4},{6,5},{7,6},{8,7},{9,8},{10,9},{11,1... | collective-permute-start | bytes 52232 | tf_op jit(solution)/shard_map/ppermute | solution.py:18
  31.2 1.1 pad_maximum_fusion.11
  32.2 1.9 collective-permute-start.2
  34.2 5.8 %collective-permute-start.3 = (f32[3,34,1,128]{3,2,1,0:T(1,128)S(1)}, f32[3,34,1,128]{3,2,1,0:T(1,128)S(1)}, u32[]{:S(2)}, u32[]{:S(2)}) collective-permute-start(f32[3,34,1,128]{3,2,1,0:T(1,128)S(1)} %get-tuple-element.62), channel_id=1, source_target_pairs={{1,0},{2,1},{3,2},{4,3},{5,4},{6,5},{7,6},{8,7},{9,8},{10,9},{11,1... | collective-permute-start | bytes 156680 | tf_op jit(solution)/shard_map/ppermute | solution.py:18
  40.1 1.6 collective-permute-done.3
  41.7 1.4 pad_maximum_fusion
  44.1 4.9 %collective-permute-start.8 = (f32[1,32,128]{2,1,0:T(8,128)S(1)}, f32[1,32,128]{2,1,0:T(8,128)S(1)}, u32[]{:S(2)}, u32[]{:S(2)}) collective-permute-start(f32[1,32,128]{2,1,0:T(8,128)S(1)} %get-tuple-element.201), channel_id=1, source_target_pairs={{0,32},{32,64},{64,96},{96,128},{128,160},{160,192},{192,224},{224... | collective-permute-start | bytes 49160 | tf_op jit(solution)/shard_map/ppermute | solution.py:17
  49.1 1.3 collective-permute-start.9
  50.4 7.8 %all-to-all-start.1 = ((f32[32,32,128]{2,1,0:T(8,128)}), f32[32,32,128]{2,1,0:T(8,128)S(1)}, u32[]{:S(2)}, u32[]{:S(2)}) async-start(f32[32,32,128]{2,1,0:T(8,128)} %param.7), calls=%async_computation.1 | async-start | bytes 1048576 | tf_op jit(solution)/shard_map/all_to_all | solution.py:109
  58.2 2.0 collective-permute-start.10
  60.3 5.6 %collective-permute-start.11 = (f32[34,1,128]{2,1,0:T(1,128)S(1)}, f32[34,1,128]{2,1,0:T(1,128)S(1)}, u32[]{:S(2)}, u32[]{:S(2)}) collective-permute-start(f32[34,1,128]{2,1,0:T(1,128)S(1)} %get-tuple-element.112), channel_id=1, source_target_pairs={{1,0},{2,1},{3,2},{4,3},{5,4},{6,5},{7,6},{8,7},{9,8},{10,9},{11,1... | collective-permute-start | bytes 52232 | tf_op jit(solution)/shard_map/ppermute | solution.py:18
  65.9 1.3 add_multiply_fusion
  68.6 4.6 %collective-permute-start.12 = (f32[1,32,128]{2,1,0:T(8,128)S(1)}, f32[1,32,128]{2,1,0:T(8,128)S(1)}, u32[]{:S(2)}, u32[]{:S(2)}) collective-permute-start(f32[1,32,128]{2,1,0:T(8,128)S(1)} %get-tuple-element.199), channel_id=1, source_target_pairs={{0,32},{32,64},{64,96},{96,128},{128,160},{160,192},{192,224},{224... | collective-permute-start | bytes 49160 | tf_op jit(solution)/shard_map/ppermute | solution.py:17
  73.1 1.3 collective-permute-start.13
  74.5 5.4 %collective-permute-done.13 = f32[1,32,128]{2,1,0:T(8,128)S(1)} collective-permute-done((f32[1,32,128]{2,1,0:T(8,128)S(1)}, f32[1,32,128]{2,1,0:T(8,128)S(1)}, u32[]{:S(2)}, u32[]{:S(2)}) %collective-permute-start.13) | collective-permute-done | bytes 16416 | tf_op jit(solution)/shard_map/ppermute | solution.py:18
  80.0 1.9 collective-permute-start.14
  81.9 5.8 %collective-permute-start.15 = (f32[34,1,128]{2,1,0:T(1,128)S(1)}, f32[34,1,128]{2,1,0:T(1,128)S(1)}, u32[]{:S(2)}, u32[]{:S(2)}) collective-permute-start(f32[34,1,128]{2,1,0:T(1,128)S(1)} %get-tuple-element.110), channel_id=1, source_target_pairs={{1,0},{2,1},{3,2},{4,3},{5,4},{6,5},{7,6},{8,7},{9,8},{10,9},{11,1... | collective-permute-start | bytes 52232 | tf_op jit(solution)/shard_map/ppermute | solution.py:18
  87.7 1.1 pad_slice_fusion.2
  90.0 3.9 %collective-permute-start.16 = (f32[1,32,128]{2,1,0:T(8,128)S(1)}, f32[1,32,128]{2,1,0:T(8,128)S(1)}, u32[]{:S(2)}, u32[]{:S(2)}) collective-permute-start(f32[1,32,128]{2,1,0:T(8,128)S(1)} %get-tuple-element.197), channel_id=1, source_target_pairs={{0,32},{32,64},{64,96},{96,128},{128,160},{160,192},{192,224},{224... | collective-permute-start | bytes 49160 | tf_op jit(solution)/shard_map/ppermute | solution.py:17
  93.9 1.3 collective-permute-start.17
  95.2 0.8 pad_slice_fusion
  96.1 4.3 %collective-permute-done.17 = f32[1,32,128]{2,1,0:T(8,128)S(1)} collective-permute-done((f32[1,32,128]{2,1,0:T(8,128)S(1)}, f32[1,32,128]{2,1,0:T(8,128)S(1)}, u32[]{:S(2)}, u32[]{:S(2)}) %collective-permute-start.17) | collective-permute-done | bytes 16416 | tf_op jit(solution)/shard_map/ppermute | solution.py:18
  100.4 1.9 collective-permute-start.18
  102.4 5.8 %collective-permute-start.19 = (f32[34,1,128]{2,1,0:T(1,128)S(1)}, f32[34,1,128]{2,1,0:T(1,128)S(1)}, u32[]{:S(2)}, u32[]{:S(2)}) collective-permute-start(f32[34,1,128]{2,1,0:T(1,128)S(1)} %get-tuple-element.108), channel_id=1, source_target_pairs={{1,0},{2,1},{3,2},{4,3},{5,4},{6,5},{7,6},{8,7},{9,8},{10,9},{11,1... | collective-permute-start | bytes 52232 | tf_op jit(solution)/shard_map/ppermute | solution.py:18
  110.2 1.1 fusion.11
  111.3 8.0 %all-to-all-start = ((f32[32,32,128]{2,1,0:T(8,128)}), f32[32,32,128]{2,1,0:T(8,128)S(1)}, u32[]{:S(2)}, u32[]{:S(2)}) async-start(f32[32,32,128]{2,1,0:T(8,128)} %fusion.11), calls=%async_computation | async-start | bytes 1048576 | tf_op jit(solution)/shard_map/all_to_all | solution.py:108
  119.5 1.1 pad_slice_fusion.5
  120.7 8.5 %all-to-all-done = f32[32,32,128]{2,1,0:T(8,128)S(1)} async-done(((f32[32,32,128]{2,1,0:T(8,128)}), f32[32,32,128]{2,1,0:T(8,128)S(1)}, u32[]{:S(2)}, u32[]{:S(2)}) %all-to-all-start) | async-done | bytes 524320 | tf_op jit(solution)/shard_map/all_to_all | solution.py:108
  129.8 0.9 copy-done.8
  138.4 1.0 add_divide_fusion
  139.4 5.4 %all-to-all-start.2 = ((f32[1,1024,128]{2,0,1:T(1,128)}), f32[1,1024,128]{2,0,1:T(1,128)S(1)}, u32[]{:S(2)}, u32[]{:S(2)}) async-start(f32[1,1024,128]{2,0,1:T(1,128)} %bitcast.8), calls=%async_computation.2 | async-start | bytes 1048576 | tf_op jit(solution)/shard_map/all_to_all | solution.py:90
  145.2 0.9 fusion.60
  146.1 8.5 %all-to-all-done.2 = f32[1,1024,128]{2,0,1:T(1,128)S(1)} async-done(((f32[1,1024,128]{2,0,1:T(1,128)}), f32[1,1024,128]{2,0,1:T(1,128)S(1)}, u32[]{:S(2)}, u32[]{:S(2)}) %all-to-all-start.2) | async-done | bytes 524320 | tf_op jit(solution)/shard_map/all_to_all | solution.py:90
  154.7 0.9 copy-done.13
  159.2 0.9 multiply_add_fusion.29
  161.0 0.8 multiply_add_fusion.27
  164.1 1.3 collective-permute-start.20
  165.4 6.4 %collective-permute-done.20 = f32[3,32,128]{2,1,0:T(8,128)S(1)} collective-permute-done((f32[3,32,128]{2,1,0:T(8,128)S(1)}, f32[3,32,128]{2,1,0:T(8,128)S(1)}, u32[]{:S(2)}, u32[]{:S(2)}) %collective-permute-start.20) | collective-permute-done | bytes 49184 | tf_op jit(solution)/shard_map/ppermute | solution.py:26
  172.5 69.8 %all-gather.3.cloned.1.call-done = f32[64,32,128]{2,1,0:T(8,128)} async-done(((f32[4,32,128]{2,1,0:T(8,128)}), f32[64,32,128]{2,1,0:T(8,128)}) %all-gather.3.cloned.1.call-update) | async-done | bytes 1048592 | tf_op jit(solution)/shard_map/all_gather | solution.py:148
  242.3 1.9 slice_bitcast_fusion.11
  247.2 0.8 pad_maximum_fusion.5
  (203 shorter events, 25.5 us)
Async XLA Ops:
  6.5 11.9 %copy-start.5 = (f32[32,32,128]{2,1,0:T(8,128)S(1)}, f32[32,32,128]{2,1,0:T(8,128)}, u32[]{:S(2)}) copy-start(f32[32,32,128]{2,1,0:T(8,128)} %param.4) | copy-start | bytes 1572868
  6.5 24.6 %copy-start.2 = (f32[32,32,128]{2,1,0:T(8,128)S(1)}, f32[32,32,128]{2,1,0:T(8,128)}, u32[]{:S(2)}) copy-start(f32[32,32,128]{2,1,0:T(8,128)} %param.5) | copy-start | bytes 1572868
  6.5 24.6 %copy-start.1 = (f32[32,32,128]{2,1,0:T(8,128)S(1)}, f32[32,32,128]{2,1,0:T(8,128)}, u32[]{:S(2)}) copy-start(f32[32,32,128]{2,1,0:T(8,128)} %param.6) | copy-start | bytes 1572868
  7.4 11.1 %collective-permute-start.4 = (f32[1,32,128]{2,1,0:T(8,128)S(1)}, f32[1,32,128]{2,1,0:T(8,128)S(1)}, u32[]{:S(2)}, u32[]{:S(2)}) collective-permute-start(f32[1,32,128]{2,1,0:T(8,128)S(1)} %get-tuple-element.204), channel_id=1, source_target_pairs={{0,32},{32,64},{64,96},{96,128},{128,160},{160,192},{192,224},{224... | collective-permute-start | bytes 49160 | tf_op jit(solution)/shard_map/ppermute | solution.py:17
  12.0 19.1 %collective-permute-start = (f32[3,1,32,128]{3,2,1,0:T(8,128)S(1)}, f32[3,1,32,128]{3,2,1,0:T(8,128)S(1)}, u32[]{:S(2)}, u32[]{:S(2)}) collective-permute-start(f32[3,1,32,128]{3,2,1,0:T(8,128)S(1)} %get-tuple-element.65), channel_id=1, source_target_pairs={{0,32},{32,64},{64,96},{96,128},{128,160},{160,192},{192,224},{224... | collective-permute-start | bytes 147464 | tf_op jit(solution)/shard_map/ppermute | solution.py:17
  15.9 15.3 %collective-permute-start.1 = (f32[3,1,32,128]{3,2,1,0:T(8,128)S(1)}, f32[3,1,32,128]{3,2,1,0:T(8,128)S(1)}, u32[]{:S(2)}, u32[]{:S(2)}) collective-permute-start(f32[3,1,32,128]{3,2,1,0:T(8,128)S(1)} %get-tuple-element.66), channel_id=1, source_target_pairs={{32,0},{64,32},{96,64},{128,96},{160,128},{192,160},{224,192},{256... | collective-permute-start | bytes 147464 | tf_op jit(solution)/shard_map/ppermute | solution.py:18
  17.2 6.3 %collective-permute-start.5 = (f32[1,32,128]{2,1,0:T(8,128)S(1)}, f32[1,32,128]{2,1,0:T(8,128)S(1)}, u32[]{:S(2)}, u32[]{:S(2)}) collective-permute-start(f32[1,32,128]{2,1,0:T(8,128)S(1)} %get-tuple-element.203), channel_id=1, source_target_pairs={{32,0},{64,32},{96,64},{128,96},{160,128},{192,160},{224,192},{256... | collective-permute-start | bytes 49160 | tf_op jit(solution)/shard_map/ppermute | solution.py:18
  23.5 16.5 %collective-permute-start.6 = (f32[34,1,128]{2,1,0:T(1,128)S(1)}, f32[34,1,128]{2,1,0:T(1,128)S(1)}, u32[]{:S(2)}, u32[]{:S(2)}) collective-permute-start(f32[34,1,128]{2,1,0:T(1,128)S(1)} %get-tuple-element.113), channel_id=1, source_target_pairs={{0,1},{1,2},{2,3},{3,4},{4,5},{5,6},{6,7},{7,8},{8,9},{9,10},{10,1... | collective-permute-start | bytes 52232 | tf_op jit(solution)/shard_map/ppermute | solution.py:17
  25.4 14.6 %collective-permute-start.7 = (f32[34,1,128]{2,1,0:T(1,128)S(1)}, f32[34,1,128]{2,1,0:T(1,128)S(1)}, u32[]{:S(2)}, u32[]{:S(2)}) collective-permute-start(f32[34,1,128]{2,1,0:T(1,128)S(1)} %get-tuple-element.114), channel_id=1, source_target_pairs={{1,0},{2,1},{3,2},{4,3},{5,4},{6,5},{7,6},{8,7},{9,8},{10,9},{11,1... | collective-permute-start | bytes 52232 | tf_op jit(solution)/shard_map/ppermute | solution.py:18
  32.2 7.8 %collective-permute-start.2 = (f32[3,34,1,128]{3,2,1,0:T(1,128)S(1)}, f32[3,34,1,128]{3,2,1,0:T(1,128)S(1)}, u32[]{:S(2)}, u32[]{:S(2)}) collective-permute-start(f32[3,34,1,128]{3,2,1,0:T(1,128)S(1)} %get-tuple-element.61), channel_id=1, source_target_pairs={{0,1},{1,2},{2,3},{3,4},{4,5},{5,6},{6,7},{7,8},{8,9},{9,10},{10,1... | collective-permute-start | bytes 156680 | tf_op jit(solution)/shard_map/ppermute | solution.py:17
  34.2 7.5 %collective-permute-start.3 = (f32[3,34,1,128]{3,2,1,0:T(1,128)S(1)}, f32[3,34,1,128]{3,2,1,0:T(1,128)S(1)}, u32[]{:S(2)}, u32[]{:S(2)}) collective-permute-start(f32[3,34,1,128]{3,2,1,0:T(1,128)S(1)} %get-tuple-element.62), channel_id=1, source_target_pairs={{1,0},{2,1},{3,2},{4,3},{5,4},{6,5},{7,6},{8,7},{9,8},{10,9},{11,1... | collective-permute-start | bytes 156680 | tf_op jit(solution)/shard_map/ppermute | solution.py:18
  44.1 14.0 %collective-permute-start.8 = (f32[1,32,128]{2,1,0:T(8,128)S(1)}, f32[1,32,128]{2,1,0:T(8,128)S(1)}, u32[]{:S(2)}, u32[]{:S(2)}) collective-permute-start(f32[1,32,128]{2,1,0:T(8,128)S(1)} %get-tuple-element.201), channel_id=1, source_target_pairs={{0,32},{32,64},{64,96},{96,128},{128,160},{160,192},{192,224},{224... | collective-permute-start | bytes 49160 | tf_op jit(solution)/shard_map/ppermute | solution.py:17
  49.1 9.1 %collective-permute-start.9 = (f32[1,32,128]{2,1,0:T(8,128)S(1)}, f32[1,32,128]{2,1,0:T(8,128)S(1)}, u32[]{:S(2)}, u32[]{:S(2)}) collective-permute-start(f32[1,32,128]{2,1,0:T(8,128)S(1)} %get-tuple-element.202), channel_id=1, source_target_pairs={{32,0},{64,32},{96,64},{128,96},{160,128},{192,160},{224,192},{256... | collective-permute-start | bytes 49160 | tf_op jit(solution)/shard_map/ppermute | solution.py:18
  50.4 60.9 %all-to-all-start.1 = ((f32[32,32,128]{2,1,0:T(8,128)}), f32[32,32,128]{2,1,0:T(8,128)S(1)}, u32[]{:S(2)}, u32[]{:S(2)}) async-start(f32[32,32,128]{2,1,0:T(8,128)} %param.7), calls=%async_computation.1 | async-start | bytes 1048576 | tf_op jit(solution)/shard_map/all_to_all | solution.py:109
  58.2 9.4 %collective-permute-start.10 = (f32[34,1,128]{2,1,0:T(1,128)S(1)}, f32[34,1,128]{2,1,0:T(1,128)S(1)}, u32[]{:S(2)}, u32[]{:S(2)}) collective-permute-start(f32[34,1,128]{2,1,0:T(1,128)S(1)} %get-tuple-element.111), channel_id=1, source_target_pairs={{0,1},{1,2},{2,3},{3,4},{4,5},{5,6},{6,7},{7,8},{8,9},{9,10},{10,1... | collective-permute-start | bytes 52232 | tf_op jit(solution)/shard_map/ppermute | solution.py:17
  60.3 7.4 %collective-permute-start.11 = (f32[34,1,128]{2,1,0:T(1,128)S(1)}, f32[34,1,128]{2,1,0:T(1,128)S(1)}, u32[]{:S(2)}, u32[]{:S(2)}) collective-permute-start(f32[34,1,128]{2,1,0:T(1,128)S(1)} %get-tuple-element.112), channel_id=1, source_target_pairs={{1,0},{2,1},{3,2},{4,3},{5,4},{6,5},{7,6},{8,7},{9,8},{10,9},{11,1... | collective-permute-start | bytes 52232 | tf_op jit(solution)/shard_map/ppermute | solution.py:18
  67.2 21.6 %copy-start.3 = (f32[31,32,128]{2,1,0:T(8,128)}, f32[31,32,128]{2,1,0:T(8,128)S(1)}, u32[]{:S(2)}) copy-start(f32[31,32,128]{2,1,0:T(8,128)S(1)} %add_multiply_fusion) | copy-start | bytes 1523716
  68.6 6.0 %collective-permute-start.12 = (f32[1,32,128]{2,1,0:T(8,128)S(1)}, f32[1,32,128]{2,1,0:T(8,128)S(1)}, u32[]{:S(2)}, u32[]{:S(2)}) collective-permute-start(f32[1,32,128]{2,1,0:T(8,128)S(1)} %get-tuple-element.199), channel_id=1, source_target_pairs={{0,32},{32,64},{64,96},{96,128},{128,160},{160,192},{192,224},{224... | collective-permute-start | bytes 49160 | tf_op jit(solution)/shard_map/ppermute | solution.py:17
  73.1 6.8 %collective-permute-start.13 = (f32[1,32,128]{2,1,0:T(8,128)S(1)}, f32[1,32,128]{2,1,0:T(8,128)S(1)}, u32[]{:S(2)}, u32[]{:S(2)}) collective-permute-start(f32[1,32,128]{2,1,0:T(8,128)S(1)} %get-tuple-element.200), channel_id=1, source_target_pairs={{32,0},{64,32},{96,64},{128,96},{160,128},{192,160},{224,192},{256... | collective-permute-start | bytes 49160 | tf_op jit(solution)/shard_map/ppermute | solution.py:18
  80.0 8.8 %collective-permute-start.14 = (f32[34,1,128]{2,1,0:T(1,128)S(1)}, f32[34,1,128]{2,1,0:T(1,128)S(1)}, u32[]{:S(2)}, u32[]{:S(2)}) collective-permute-start(f32[34,1,128]{2,1,0:T(1,128)S(1)} %get-tuple-element.109), channel_id=1, source_target_pairs={{0,1},{1,2},{2,3},{3,4},{4,5},{5,6},{6,7},{7,8},{8,9},{9,10},{10,1... | collective-permute-start | bytes 52232 | tf_op jit(solution)/shard_map/ppermute | solution.py:17
  81.9 7.2 %collective-permute-start.15 = (f32[34,1,128]{2,1,0:T(1,128)S(1)}, f32[34,1,128]{2,1,0:T(1,128)S(1)}, u32[]{:S(2)}, u32[]{:S(2)}) collective-permute-start(f32[34,1,128]{2,1,0:T(1,128)S(1)} %get-tuple-element.110), channel_id=1, source_target_pairs={{1,0},{2,1},{3,2},{4,3},{5,4},{6,5},{7,6},{8,7},{9,8},{10,9},{11,1... | collective-permute-start | bytes 52232 | tf_op jit(solution)/shard_map/ppermute | solution.py:18
  90.0 6.1 %collective-permute-start.16 = (f32[1,32,128]{2,1,0:T(8,128)S(1)}, f32[1,32,128]{2,1,0:T(8,128)S(1)}, u32[]{:S(2)}, u32[]{:S(2)}) collective-permute-start(f32[1,32,128]{2,1,0:T(8,128)S(1)} %get-tuple-element.197), channel_id=1, source_target_pairs={{0,32},{32,64},{64,96},{96,128},{128,160},{160,192},{192,224},{224... | collective-permute-start | bytes 49160 | tf_op jit(solution)/shard_map/ppermute | solution.py:17
  93.9 6.5 %collective-permute-start.17 = (f32[1,32,128]{2,1,0:T(8,128)S(1)}, f32[1,32,128]{2,1,0:T(8,128)S(1)}, u32[]{:S(2)}, u32[]{:S(2)}) collective-permute-start(f32[1,32,128]{2,1,0:T(8,128)S(1)} %get-tuple-element.198), channel_id=1, source_target_pairs={{32,0},{64,32},{96,64},{128,96},{160,128},{192,160},{224,192},{256... | collective-permute-start | bytes 49160 | tf_op jit(solution)/shard_map/ppermute | solution.py:18
  100.4 8.4 %collective-permute-start.18 = (f32[34,1,128]{2,1,0:T(1,128)S(1)}, f32[34,1,128]{2,1,0:T(1,128)S(1)}, u32[]{:S(2)}, u32[]{:S(2)}) collective-permute-start(f32[34,1,128]{2,1,0:T(1,128)S(1)} %get-tuple-element.107), channel_id=1, source_target_pairs={{0,1},{1,2},{2,3},{3,4},{4,5},{5,6},{6,7},{7,8},{8,9},{9,10},{10,1... | collective-permute-start | bytes 52232 | tf_op jit(solution)/shard_map/ppermute | solution.py:17
  102.4 7.2 %collective-permute-start.19 = (f32[34,1,128]{2,1,0:T(1,128)S(1)}, f32[34,1,128]{2,1,0:T(1,128)S(1)}, u32[]{:S(2)}, u32[]{:S(2)}) collective-permute-start(f32[34,1,128]{2,1,0:T(1,128)S(1)} %get-tuple-element.108), channel_id=1, source_target_pairs={{1,0},{2,1},{3,2},{4,3},{5,4},{6,5},{7,6},{8,7},{9,8},{10,9},{11,1... | collective-permute-start | bytes 52232 | tf_op jit(solution)/shard_map/ppermute | solution.py:18
  111.3 17.8 %all-to-all-start = ((f32[32,32,128]{2,1,0:T(8,128)}), f32[32,32,128]{2,1,0:T(8,128)S(1)}, u32[]{:S(2)}, u32[]{:S(2)}) async-start(f32[32,32,128]{2,1,0:T(8,128)} %fusion.11), calls=%async_computation | async-start | bytes 1048576 | tf_op jit(solution)/shard_map/all_to_all | solution.py:108
  129.6 1.0 copy-start.8
  129.6 1.2 copy-start.9
  138.3 6.8 %copy-start.4 = (f32[31,32,128]{2,1,0:T(8,128)S(1)}, f32[31,32,128]{2,1,0:T(8,128)}, u32[]{:S(2)}) copy-start(f32[31,32,128]{2,1,0:T(8,128)} %copy-done.3) | copy-start | bytes 1523716
  139.4 15.2 %all-to-all-start.2 = ((f32[1,1024,128]{2,0,1:T(1,128)}), f32[1,1024,128]{2,0,1:T(1,128)S(1)}, u32[]{:S(2)}, u32[]{:S(2)}) async-start(f32[1,1024,128]{2,0,1:T(1,128)} %bitcast.8), calls=%async_computation.2 | async-start | bytes 1048576 | tf_op jit(solution)/shard_map/all_to_all | solution.py:90
  144.8 97.5 %all-gather.3.cloned.1.call-start = ((), (), s32[]{:S(2)}) async-start(), calls=%async_computation.3 | async-start | bytes 1114112 | tf_op jit(solution)/shard_map/all_gather | solution.py:148
  154.6 1.0 copy-start.13
  156.2 1.0 copy-start.10
  156.2 1.2 copy-start.11
  156.3 1.3 copy-start.12
  163.6 8.2 %copy-start.6 = (f32[31,32,128]{2,1,0:T(8,128)}, f32[31,32,128]{2,1,0:T(8,128)S(1)}, u32[]{:S(2)}) copy-start(f32[31,32,128]{2,1,0:T(8,128)S(1)} %get-tuple-element.60) | copy-start | bytes 1523716
  164.1 7.7 %collective-permute-start.20 = (f32[3,32,128]{2,1,0:T(8,128)S(1)}, f32[3,32,128]{2,1,0:T(8,128)S(1)}, u32[]{:S(2)}, u32[]{:S(2)}) collective-permute-start(f32[3,32,128]{2,1,0:T(8,128)S(1)} %pad_maximum_fusion.15), channel_id=1, source_target_pairs={{32,0},{64,32},{96,64},{128,96},{160,128},{192,160},{224,192},{256... | collective-permute-start | bytes 147464 | tf_op jit(solution)/shard_map/ppermute | solution.py:26
  242.3 2.0 copy-start
  245.9 1.0 copy-start.7
Sparse Core Ops, SparseCore 0:
  172.6 69.6 all-gather.2
where the time goes:
time: 256 us; the launch traced here: 255 us
  waiting for transfers between devices  111 us (43%)
  starting transfers between devices  88.6 us (35%)
  other arithmetic  24.4 us (10%)
  local copies, waits for them, and re-layouts  16.1 us (6%)
  between operations  14.8 us (6%)
    all_gather x1, waiting for transfers between devices, local(): collected = lax.all_gather(equations[None], 'gz', axis=0, tiled=True)  69.8 us
    ppermute x10, starting transfers between devices, padded_2(): after = lax.ppermute(leading, axis, down)  35.1 us
    ppermute x10, starting transfers between devices, padded_2(): before = lax.ppermute(last, axis, up)  30.7 us
    ppermute x10, waiting for transfers between devices, padded_2(): after = lax.ppermute(leading, axis, down)  17.3 us
    all_to_all x1, waiting for transfers between devices, solve_rows(): return lax.all_to_all(solved, 'gy', split_axis=1, concat_axis=0, tiled=True)  8.48 us
    all_to_all x1, waiting for transfers between devices, local(): lax.all_to_all(state, 'gy', split_axis=0, concat_axis=1, tiled=True)  8.45 us
    all_to_all x1, starting transfers between devices, local(): lax.all_to_all(state, 'gy', split_axis=0, concat_axis=1, tiled=True)  8.02 us
    all_to_all x1, starting transfers between devices, local(): lax.all_to_all(kappa, 'gy', split_axis=0, concat_axis=1, tiled=True)  7.77 us
  transfers between devices with their start and end apart: 25, of which 12 were waited for; matrix products, arithmetic and copies ran while one was open for 5% of the time, Pallas kernels for 0%

commit v1 on v0

--- a/solution.py
+++ b/solution.py
@@ -5,6 +5,27 @@
 
 NSUB = 4
 rate_const = 500.0
+
+
+def ring_gather(value, axis, dim):
+    size, position, rows = (lax.axis_size(axis), lax.axis_index(axis), value.shape[dim])
+    upward = [(i, (i + 1) % size) for i in range(size)]
+    left = [(i, (i - 1) % size) for i in range(size)]
+    out = jnp.zeros((*value.shape[:dim], size * rows, *value.shape[dim + 1 :]), value.dtype)
+    out = lax.dynamic_update_slice_in_dim(out, value, position * rows, axis=dim)
+    from_left = from_right = value
+    half = size // 2
+    for hop in range(1, half + 1):
+        from_left = lax.ppermute(from_left, axis, upward)
+        out = lax.dynamic_update_slice_in_dim(
+            out, from_left, (position - hop) % size * rows, axis=dim
+        )
+        if hop < size - half:
+            from_right = lax.ppermute(from_right, axis, left)
+            out = lax.dynamic_update_slice_in_dim(
+                out, from_right, (position + hop) % size * rows, axis=dim
+            )
+    return out
 
 
 def padded_2(x, sides, width):
@@ -145,7 +166,7 @@
     sup_red = -sep_high * following[2]
     rhs_red = lines[depth_z - 1] + sep_low * base[inner_count - 1] + sep_high * following[0]
     equations = jnp.stack([sub_red, diag_red, sup_red, rhs_red])
-    collected = lax.all_gather(equations[None], "gz", axis=0, tiled=True)
+    collected = ring_gather(equations[None], "gz", 0)
     values = reduce_lines(collected[:, 0], collected[:, 1], collected[:, 2], (collected[:, 3],), 0)[
         0
     ]

time: 256 us -> 231 us (0.902)
  the two profiles are of different devices: /device:TPU:2 before, /device:TPU:128 now
where the time goes in v1:
time: 231 us; the launch traced here: 229 us
  starting transfers between devices  144 us (62%)
  waiting for transfers between devices  43.9 us (19%)
  other arithmetic  24.5 us (11%)
  local copies, waits for them, and re-layouts  14.9 us (6%)
    ppermute x10, starting transfers between devices, padded_2(): before = lax.ppermute(last, axis, up)  33.2 us
    ppermute x7, starting transfers between devices, ring_gather(): from_right = lax.ppermute(from_right, axis, left)  33.1 us
    ppermute x10, starting transfers between devices, padded_2(): after = lax.ppermute(leading, axis, down)  22.8 us
    ppermute x8, starting transfers between devices, ring_gather(): from_left = lax.ppermute(from_left, axis, upward)  18.1 us
    all_to_all x1, starting transfers between devices, local(): lax.all_to_all(state, 'gy', split_axis=0, concat_axis=1, tiled=True)  15.4 us
    ppermute x10, waiting for transfers between devices, padded_2(): after = lax.ppermute(leading, axis, down)  14.5 us
    all_to_all x1, starting transfers between devices, local(): lax.all_to_all(kappa, 'gy', split_axis=0, concat_axis=1, tiled=True)  12.5 us
    all_to_all x1, waiting for transfers between devices, solve_rows(): return lax.all_to_all(solved, 'gy', split_axis=1, concat_axis=0, tiled=True)  9.82 us
  transfers between devices with their start and end apart: 39, of which 18 were waited for; matrix products, arithmetic and copies ran while one was open for 5% of the time, Pallas kernels for 0%

profile of v1, /device:TPU:128, one launch (start us, length us, event | category | flops | bytes accessed | tf_op | source)
XLA Modules:
  0.0 229.1 jit_solution(15674321954106391350)
XLA Ops:
  0.9 3.8 %collective-permute-start.4 = (f32[1,32,128]{2,1,0:T(8,128)S(1)}, f32[1,32,128]{2,1,0:T(8,128)S(1)}, u32[]{:S(2)}, u32[]{:S(2)}) collective-permute-start(f32[1,32,128]{2,1,0:T(8,128)S(1)} %get-tuple-element.204), channel_id=1, source_target_pairs={{0,32},{32,64},{64,96},{96,128},{128,160},{160,192},{192,224},{224... | collective-permute-start | bytes 49160 | tf_op jit(solution)/shard_map/ppermute | solution.py:38
  5.5 3.8 %collective-permute-start = (f32[3,1,32,128]{3,2,1,0:T(8,128)S(1)}, f32[3,1,32,128]{3,2,1,0:T(8,128)S(1)}, u32[]{:S(2)}, u32[]{:S(2)}) collective-permute-start(f32[3,1,32,128]{3,2,1,0:T(8,128)S(1)} %get-tuple-element.65), channel_id=1, source_target_pairs={{0,32},{32,64},{64,96},{96,128},{128,160},{160,192},{192,224},{224... | collective-permute-start | bytes 147464 | tf_op jit(solution)/shard_map/ppermute | solution.py:38
  9.3 3.2 %collective-permute-start.1 = (f32[3,1,32,128]{3,2,1,0:T(8,128)S(1)}, f32[3,1,32,128]{3,2,1,0:T(8,128)S(1)}, u32[]{:S(2)}, u32[]{:S(2)}) collective-permute-start(f32[3,1,32,128]{3,2,1,0:T(8,128)S(1)} %get-tuple-element.66), channel_id=1, source_target_pairs={{32,0},{64,32},{96,64},{128,96},{160,128},{192,160},{224,192},{256... | collective-permute-start | bytes 147464 | tf_op jit(solution)/shard_map/ppermute | solution.py:39
  12.6 2.0 collective-permute-start.5
  14.7 3.5 %collective-permute-done.5 = f32[1,32,128]{2,1,0:T(8,128)S(1)} collective-permute-done((f32[1,32,128]{2,1,0:T(8,128)S(1)}, f32[1,32,128]{2,1,0:T(8,128)S(1)}, u32[]{:S(2)}, u32[]{:S(2)}) %collective-permute-start.5) | collective-permute-done | bytes 16416 | tf_op jit(solution)/shard_map/ppermute | solution.py:39
  19.5 1.3 collective-permute-start.7
  21.9 4.8 %collective-permute-start.2 = (f32[3,34,1,128]{3,2,1,0:T(1,128)S(1)}, f32[3,34,1,128]{3,2,1,0:T(1,128)S(1)}, u32[]{:S(2)}, u32[]{:S(2)}) collective-permute-start(f32[3,34,1,128]{3,2,1,0:T(1,128)S(1)} %get-tuple-element.61), channel_id=1, source_target_pairs={{0,1},{1,2},{2,3},{3,4},{4,5},{5,6},{6,7},{7,8},{8,9},{9,10},{10,1... | collective-permute-start | bytes 156680 | tf_op jit(solution)/shard_map/ppermute | solution.py:38
  26.8 1.3 collective-permute-start.3
  28.2 2.9 %collective-permute-done.3 = f32[3,34,1,128]{3,2,1,0:T(1,128)S(1)} collective-permute-done((f32[3,34,1,128]{3,2,1,0:T(1,128)S(1)}, f32[3,34,1,128]{3,2,1,0:T(1,128)S(1)}, u32[]{:S(2)}, u32[]{:S(2)}) %collective-permute-start.3) | collective-permute-done | bytes 52256 | tf_op jit(solution)/shard_map/ppermute | solution.py:39
  31.1 1.4 pad_maximum_fusion
  33.6 3.6 %collective-permute-start.8 = (f32[1,32,128]{2,1,0:T(8,128)S(1)}, f32[1,32,128]{2,1,0:T(8,128)S(1)}, u32[]{:S(2)}, u32[]{:S(2)}) collective-permute-start(f32[1,32,128]{2,1,0:T(8,128)S(1)} %get-tuple-element.201), channel_id=1, source_target_pairs={{0,32},{32,64},{64,96},{96,128},{128,160},{160,192},{192,224},{224... | collective-permute-start | bytes 49160 | tf_op jit(solution)/shard_map/ppermute | solution.py:38
  37.2 3.4 %collective-permute-start.9 = (f32[1,32,128]{2,1,0:T(8,128)S(1)}, f32[1,32,128]{2,1,0:T(8,128)S(1)}, u32[]{:S(2)}, u32[]{:S(2)}) collective-permute-start(f32[1,32,128]{2,1,0:T(8,128)S(1)} %get-tuple-element.202), channel_id=1, source_target_pairs={{32,0},{64,32},{96,64},{128,96},{160,128},{192,160},{224,192},{256... | collective-permute-start | bytes 49160 | tf_op jit(solution)/shard_map/ppermute | solution.py:39
  40.7 12.5 %all-to-all-start.1 = ((f32[32,32,128]{2,1,0:T(8,128)}), f32[32,32,128]{2,1,0:T(8,128)S(1)}, u32[]{:S(2)}, u32[]{:S(2)}) async-start(f32[32,32,128]{2,1,0:T(8,128)} %param.7), calls=%async_computation.1 | async-start | bytes 1048576 | tf_op jit(solution)/shard_map/all_to_all | solution.py:130
  53.2 2.2 collective-permute-start.10
  55.4 1.3 collective-permute-start.11
  58.0 1.6 collective-permute-done.11
  60.6 2.7 %collective-permute-start.12 = (f32[1,32,128]{2,1,0:T(8,128)S(1)}, f32[1,32,128]{2,1,0:T(8,128)S(1)}, u32[]{:S(2)}, u32[]{:S(2)}) collective-permute-start(f32[1,32,128]{2,1,0:T(8,128)S(1)} %get-tuple-element.199), channel_id=1, source_target_pairs={{0,32},{32,64},{64,96},{96,128},{128,160},{160,192},{192,224},{224... | collective-permute-start | bytes 49160 | tf_op jit(solution)/shard_map/ppermute | solution.py:38
  63.3 4.4 %collective-permute-start.13 = (f32[1,32,128]{2,1,0:T(8,128)S(1)}, f32[1,32,128]{2,1,0:T(8,128)S(1)}, u32[]{:S(2)}, u32[]{:S(2)}) collective-permute-start(f32[1,32,128]{2,1,0:T(8,128)S(1)} %get-tuple-element.200), channel_id=1, source_target_pairs={{32,0},{64,32},{96,64},{128,96},{160,128},{192,160},{224,192},{256... | collective-permute-start | bytes 49160 | tf_op jit(solution)/shard_map/ppermute | solution.py:39
  67.7 2.4 %collective-permute-done.13 = f32[1,32,128]{2,1,0:T(8,128)S(1)} collective-permute-done((f32[1,32,128]{2,1,0:T(8,128)S(1)}, f32[1,32,128]{2,1,0:T(8,128)S(1)}, u32[]{:S(2)}, u32[]{:S(2)}) %collective-permute-start.13) | collective-permute-done | bytes 16416 | tf_op jit(solution)/shard_map/ppermute | solution.py:39
  70.1 4.1 %collective-permute-start.14 = (f32[34,1,128]{2,1,0:T(1,128)S(1)}, f32[34,1,128]{2,1,0:T(1,128)S(1)}, u32[]{:S(2)}, u32[]{:S(2)}) collective-permute-start(f32[34,1,128]{2,1,0:T(1,128)S(1)} %get-tuple-element.109), channel_id=1, source_target_pairs={{0,1},{1,2},{2,3},{3,4},{4,5},{5,6},{6,7},{7,8},{8,9},{9,10},{10,1... | collective-permute-start | bytes 52232 | tf_op jit(solution)/shard_map/ppermute | solution.py:38
  74.3 1.3 collective-permute-start.15
  78.3 3.7 %collective-permute-start.16 = (f32[1,32,128]{2,1,0:T(8,128)S(1)}, f32[1,32,128]{2,1,0:T(8,128)S(1)}, u32[]{:S(2)}, u32[]{:S(2)}) collective-permute-start(f32[1,32,128]{2,1,0:T(8,128)S(1)} %get-tuple-element.197), channel_id=1, source_target_pairs={{0,32},{32,64},{64,96},{96,128},{128,160},{160,192},{192,224},{224... | collective-permute-start | bytes 49160 | tf_op jit(solution)/shard_map/ppermute | solution.py:38
  82.0 3.3 %collective-permute-start.17 = (f32[1,32,128]{2,1,0:T(8,128)S(1)}, f32[1,32,128]{2,1,0:T(8,128)S(1)}, u32[]{:S(2)}, u32[]{:S(2)}) collective-permute-start(f32[1,32,128]{2,1,0:T(8,128)S(1)} %get-tuple-element.198), channel_id=1, source_target_pairs={{32,0},{64,32},{96,64},{128,96},{160,128},{192,160},{224,192},{256... | collective-permute-start | bytes 49160 | tf_op jit(solution)/shard_map/ppermute | solution.py:39
  86.2 1.6 collective-permute-done.17
  87.8 3.0 %collective-permute-start.18 = (f32[34,1,128]{2,1,0:T(1,128)S(1)}, f32[34,1,128]{2,1,0:T(1,128)S(1)}, u32[]{:S(2)}, u32[]{:S(2)}) collective-permute-start(f32[34,1,128]{2,1,0:T(1,128)S(1)} %get-tuple-element.107), channel_id=1, source_target_pairs={{0,1},{1,2},{2,3},{3,4},{4,5},{5,6},{6,7},{7,8},{8,9},{9,10},{10,1... | collective-permute-start | bytes 52232 | tf_op jit(solution)/shard_map/ppermute | solution.py:38
  92.9 1.8 collective-permute-done.19
  96.4 15.4 %all-to-all-start = ((f32[32,32,128]{2,1,0:T(8,128)}), f32[32,32,128]{2,1,0:T(8,128)S(1)}, u32[]{:S(2)}, u32[]{:S(2)}) async-start(f32[32,32,128]{2,1,0:T(8,128)} %fusion.11), calls=%async_computation | async-start | bytes 1048576 | tf_op jit(solution)/shard_map/all_to_all | solution.py:129
  113.2 9.6 %all-to-all-done = f32[32,32,128]{2,1,0:T(8,128)S(1)} async-done(((f32[32,32,128]{2,1,0:T(8,128)}), f32[32,32,128]{2,1,0:T(8,128)S(1)}, u32[]{:S(2)}, u32[]{:S(2)}) %all-to-all-start) | async-done | bytes 524320 | tf_op jit(solution)/shard_map/all_to_all | solution.py:129
  133.0 4.4 %all-to-all-start.2 = ((f32[1,1024,128]{2,0,1:T(1,128)}), f32[1,1024,128]{2,0,1:T(1,128)S(1)}, u32[]{:S(2)}, u32[]{:S(2)}) async-start(f32[1,1024,128]{2,0,1:T(1,128)} %bitcast.8), calls=%async_computation.2 | async-start | bytes 1048576 | tf_op jit(solution)/shard_map/all_to_all | solution.py:111
  138.4 9.8 %all-to-all-done.2 = f32[1,1024,128]{2,0,1:T(1,128)S(1)} async-done(((f32[1,1024,128]{2,0,1:T(1,128)}), f32[1,1024,128]{2,0,1:T(1,128)S(1)}, u32[]{:S(2)}, u32[]{:S(2)}) %all-to-all-start.2) | async-done | bytes 524320 | tf_op jit(solution)/shard_map/all_to_all | solution.py:111
  158.0 4.3 %collective-permute-start.20 = (f32[3,32,128]{2,1,0:T(8,128)S(1)}, f32[3,32,128]{2,1,0:T(8,128)S(1)}, u32[]{:S(2)}, u32[]{:S(2)}) collective-permute-start(f32[3,32,128]{2,1,0:T(8,128)S(1)} %pad_maximum_fusion.15), channel_id=1, source_target_pairs={{32,0},{64,32},{96,64},{128,96},{160,128},{192,160},{224,192},{256... | collective-permute-start | bytes 147464 | tf_op jit(solution)/shard_map/ppermute | solution.py:47
  162.6 2.9 %collective-permute-done.20 = f32[3,32,128]{2,1,0:T(8,128)S(1)} collective-permute-done((f32[3,32,128]{2,1,0:T(8,128)S(1)}, f32[3,32,128]{2,1,0:T(8,128)S(1)}, u32[]{:S(2)}, u32[]{:S(2)}) %collective-permute-start.20) | collective-permute-done | bytes 49184 | tf_op jit(solution)/shard_map/ppermute | solution.py:47
  166.3 3.9 %collective-permute-start.21 = (f32[1,4,32,128]{3,2,1,0:T(8,128)S(1)}, f32[1,4,32,128]{3,2,1,0:T(8,128)S(1)}, u32[]{:S(2)}, u32[]{:S(2)}) collective-permute-start(f32[1,4,32,128]{3,2,1,0:T(8,128)S(1)} %fusion.34), channel_id=1, source_target_pairs={{0,32},{32,64},{64,96},{96,128},{128,160},{160,192},{192,224},{224... | collective-permute-start | bytes 196616 | tf_op jit(solution)/shard_map/ppermute | solution.py:19
  170.2 3.1 %collective-permute-start.22 = (f32[1,4,32,128]{3,2,1,0:T(8,128)S(1)}, f32[1,4,32,128]{3,2,1,0:T(8,128)S(1)}, u32[]{:S(2)}, u32[]{:S(2)}) collective-permute-start(f32[1,4,32,128]{3,2,1,0:T(8,128)S(1)} %fusion.34), channel_id=1, source_target_pairs={{0,480},{32,0},{64,32},{96,64},{128,96},{160,128},{192,160},{224,1... | collective-permute-start | bytes 196616 | tf_op jit(solution)/shard_map/ppermute | solution.py:24
  173.7 2.7 %collective-permute-start.23 = (f32[1,4,32,128]{3,2,1,0:T(8,128)S(1)}, f32[1,4,32,128]{3,2,1,0:T(8,128)S(1)}, u32[]{:S(2)}, u32[]{:S(2)}) collective-permute-start(f32[1,4,32,128]{3,2,1,0:T(8,128)S(1)} %collective-permute-done.21), channel_id=1, source_target_pairs={{0,32},{32,64},{64,96},{96,128},{128,160},{160,192},{192,224},{224... | collective-permute-start | bytes 196616 | tf_op jit(solution)/shard_map/ppermute | solution.py:19
  176.4 4.3 %collective-permute-start.24 = (f32[1,4,32,128]{3,2,1,0:T(8,128)S(1)}, f32[1,4,32,128]{3,2,1,0:T(8,128)S(1)}, u32[]{:S(2)}, u32[]{:S(2)}) collective-permute-start(f32[1,4,32,128]{3,2,1,0:T(8,128)S(1)} %collective-permute-done.22), channel_id=1, source_target_pairs={{0,480},{32,0},{64,32},{96,64},{128,96},{160,128},{192,160},{224,1... | collective-permute-start | bytes 196616 | tf_op jit(solution)/shard_map/ppermute | solution.py:24
  181.0 1.9 collective-permute-start.25
  182.9 5.1 %collective-permute-start.26 = (f32[1,4,32,128]{3,2,1,0:T(8,128)S(1)}, f32[1,4,32,128]{3,2,1,0:T(8,128)S(1)}, u32[]{:S(2)}, u32[]{:S(2)}) collective-permute-start(f32[1,4,32,128]{3,2,1,0:T(8,128)S(1)} %collective-permute-done.24), channel_id=1, source_target_pairs={{0,480},{32,0},{64,32},{96,64},{128,96},{160,128},{192,160},{224,1... | collective-permute-start | bytes 196616 | tf_op jit(solution)/shard_map/ppermute | solution.py:24
  188.4 1.9 collective-permute-start.27
  190.3 5.1 %collective-permute-start.28 = (f32[1,4,32,128]{3,2,1,0:T(8,128)S(1)}, f32[1,4,32,128]{3,2,1,0:T(8,128)S(1)}, u32[]{:S(2)}, u32[]{:S(2)}) collective-permute-start(f32[1,4,32,128]{3,2,1,0:T(8,128)S(1)} %collective-permute-done.26), channel_id=1, source_target_pairs={{0,480},{32,0},{64,32},{96,64},{128,96},{160,128},{192,160},{224,1... | collective-permute-start | bytes 196616 | tf_op jit(solution)/shard_map/ppermute | solution.py:24
  195.7 1.9 collective-permute-start.29
  197.7 5.1 %collective-permute-start.30 = (f32[1,4,32,128]{3,2,1,0:T(8,128)S(1)}, f32[1,4,32,128]{3,2,1,0:T(8,128)S(1)}, u32[]{:S(2)}, u32[]{:S(2)}) collective-permute-start(f32[1,4,32,128]{3,2,1,0:T(8,128)S(1)} %collective-permute-done.28), channel_id=1, source_target_pairs={{0,480},{32,0},{64,32},{96,64},{128,96},{160,128},{192,160},{224,1... | collective-permute-start | bytes 196616 | tf_op jit(solution)/shard_map/ppermute | solution.py:24
  203.1 1.9 collective-permute-start.31
  205.0 5.1 %collective-permute-start.32 = (f32[1,4,32,128]{3,2,1,0:T(8,128)S(1)}, f32[1,4,32,128]{3,2,1,0:T(8,128)S(1)}, u32[]{:S(2)}, u32[]{:S(2)}) collective-permute-start(f32[1,4,32,128]{3,2,1,0:T(8,128)S(1)} %collective-permute-done.30), channel_id=1, source_target_pairs={{0,480},{32,0},{64,32},{96,64},{128,96},{160,128},{192,160},{224,1... | collective-permute-start | bytes 196616 | tf_op jit(solution)/shard_map/ppermute | solution.py:24
  210.5 1.9 collective-permute-start.33
  212.4 5.1 %collective-permute-start.34 = (f32[1,4,32,128]{3,2,1,0:T(8,128)S(1)}, f32[1,4,32,128]{3,2,1,0:T(8,128)S(1)}, u32[]{:S(2)}, u32[]{:S(2)}) collective-permute-start(f32[1,4,32,128]{3,2,1,0:T(8,128)S(1)} %collective-permute-done.32), channel_id=1, source_target_pairs={{0,480},{32,0},{64,32},{96,64},{128,96},{160,128},{192,160},{224,1... | collective-permute-start | bytes 196616 | tf_op jit(solution)/shard_map/ppermute | solution.py:24
  217.8 1.9 collective-permute-start.35
  219.8 5.4 %collective-permute-done.35 = f32[1,4,32,128]{3,2,1,0:T(8,128)S(1)} collective-permute-done((f32[1,4,32,128]{3,2,1,0:T(8,128)S(1)}, f32[1,4,32,128]{3,2,1,0:T(8,128)S(1)}, u32[]{:S(2)}, u32[]{:S(2)}) %collective-permute-start.35) | collective-permute-done | bytes 65568 | tf_op jit(solution)/shard_map/ppermute | solution.py:19
  (245 shorter events, 43.0 us)
Async XLA Ops:
  0.0 14.6 %copy-start.4 = (f32[32,32,128]{2,1,0:T(8,128)S(1)}, f32[32,32,128]{2,1,0:T(8,128)}, u32[]{:S(2)}) copy-start(f32[32,32,128]{2,1,0:T(8,128)} %param.4) | copy-start | bytes 1572868
  0.0 20.9 %copy-start.1 = (f32[32,32,128]{2,1,0:T(8,128)S(1)}, f32[32,32,128]{2,1,0:T(8,128)}, u32[]{:S(2)}) copy-start(f32[32,32,128]{2,1,0:T(8,128)} %param.5) | copy-start | bytes 1572868
  0.0 20.9 %copy-start = (f32[32,32,128]{2,1,0:T(8,128)S(1)}, f32[32,32,128]{2,1,0:T(8,128)}, u32[]{:S(2)}) copy-start(f32[32,32,128]{2,1,0:T(8,128)} %param.6) | copy-start | bytes 1572868
  0.9 13.7 %collective-permute-start.4 = (f32[1,32,128]{2,1,0:T(8,128)S(1)}, f32[1,32,128]{2,1,0:T(8,128)S(1)}, u32[]{:S(2)}, u32[]{:S(2)}) collective-permute-start(f32[1,32,128]{2,1,0:T(8,128)S(1)} %get-tuple-element.204), channel_id=1, source_target_pairs={{0,32},{32,64},{64,96},{96,128},{128,160},{160,192},{192,224},{224... | collective-permute-start | bytes 49160 | tf_op jit(solution)/shard_map/ppermute | solution.py:38
  5.5 15.3 %collective-permute-start = (f32[3,1,32,128]{3,2,1,0:T(8,128)S(1)}, f32[3,1,32,128]{3,2,1,0:T(8,128)S(1)}, u32[]{:S(2)}, u32[]{:S(2)}) collective-permute-start(f32[3,1,32,128]{3,2,1,0:T(8,128)S(1)} %get-tuple-element.65), channel_id=1, source_target_pairs={{0,32},{32,64},{64,96},{96,128},{128,160},{160,192},{192,224},{224... | collective-permute-start | bytes 147464 | tf_op jit(solution)/shard_map/ppermute | solution.py:38
  9.3 11.5 %collective-permute-start.1 = (f32[3,1,32,128]{3,2,1,0:T(8,128)S(1)}, f32[3,1,32,128]{3,2,1,0:T(8,128)S(1)}, u32[]{:S(2)}, u32[]{:S(2)}) collective-permute-start(f32[3,1,32,128]{3,2,1,0:T(8,128)S(1)} %get-tuple-element.66), channel_id=1, source_target_pairs={{32,0},{64,32},{96,64},{128,96},{160,128},{192,160},{224,192},{256... | collective-permute-start | bytes 147464 | tf_op jit(solution)/shard_map/ppermute | solution.py:39
  12.6 5.6 %collective-permute-start.5 = (f32[1,32,128]{2,1,0:T(8,128)S(1)}, f32[1,32,128]{2,1,0:T(8,128)S(1)}, u32[]{:S(2)}, u32[]{:S(2)}) collective-permute-start(f32[1,32,128]{2,1,0:T(8,128)S(1)} %get-tuple-element.203), channel_id=1, source_target_pairs={{32,0},{64,32},{96,64},{128,96},{160,128},{192,160},{224,192},{256... | collective-permute-start | bytes 49160 | tf_op jit(solution)/shard_map/ppermute | solution.py:39
  18.2 9.9 %collective-permute-start.6 = (f32[34,1,128]{2,1,0:T(1,128)S(1)}, f32[34,1,128]{2,1,0:T(1,128)S(1)}, u32[]{:S(2)}, u32[]{:S(2)}) collective-permute-start(f32[34,1,128]{2,1,0:T(1,128)S(1)} %get-tuple-element.113), channel_id=1, source_target_pairs={{0,1},{1,2},{2,3},{3,4},{4,5},{5,6},{6,7},{7,8},{8,9},{9,10},{10,1... | collective-permute-start | bytes 52232 | tf_op jit(solution)/shard_map/ppermute | solution.py:38
  19.5 8.6 %collective-permute-start.7 = (f32[34,1,128]{2,1,0:T(1,128)S(1)}, f32[34,1,128]{2,1,0:T(1,128)S(1)}, u32[]{:S(2)}, u32[]{:S(2)}) collective-permute-start(f32[34,1,128]{2,1,0:T(1,128)S(1)} %get-tuple-element.114), channel_id=1, source_target_pairs={{1,0},{2,1},{3,2},{4,3},{5,4},{6,5},{7,6},{8,7},{9,8},{10,9},{11,1... | collective-permute-start | bytes 52232 | tf_op jit(solution)/shard_map/ppermute | solution.py:39
  21.9 6.3 %collective-permute-start.2 = (f32[3,34,1,128]{3,2,1,0:T(1,128)S(1)}, f32[3,34,1,128]{3,2,1,0:T(1,128)S(1)}, u32[]{:S(2)}, u32[]{:S(2)}) collective-permute-start(f32[3,34,1,128]{3,2,1,0:T(1,128)S(1)} %get-tuple-element.61), channel_id=1, source_target_pairs={{0,1},{1,2},{2,3},{3,4},{4,5},{5,6},{6,7},{7,8},{8,9},{9,10},{10,1... | collective-permute-start | bytes 156680 | tf_op jit(solution)/shard_map/ppermute | solution.py:38
  26.8 4.4 %collective-permute-start.3 = (f32[3,34,1,128]{3,2,1,0:T(1,128)S(1)}, f32[3,34,1,128]{3,2,1,0:T(1,128)S(1)}, u32[]{:S(2)}, u32[]{:S(2)}) collective-permute-start(f32[3,34,1,128]{3,2,1,0:T(1,128)S(1)} %get-tuple-element.62), channel_id=1, source_target_pairs={{1,0},{2,1},{3,2},{4,3},{5,4},{6,5},{7,6},{8,7},{9,8},{10,9},{11,1... | collective-permute-start | bytes 156680 | tf_op jit(solution)/shard_map/ppermute | solution.py:39
  33.6 19.6 %collective-permute-start.8 = (f32[1,32,128]{2,1,0:T(8,128)S(1)}, f32[1,32,128]{2,1,0:T(8,128)S(1)}, u32[]{:S(2)}, u32[]{:S(2)}) collective-permute-start(f32[1,32,128]{2,1,0:T(8,128)S(1)} %get-tuple-element.201), channel_id=1, source_target_pairs={{0,32},{32,64},{64,96},{96,128},{128,160},{160,192},{192,224},{224... | collective-permute-start | bytes 49160 | tf_op jit(solution)/shard_map/ppermute | solution.py:38
  37.2 16.0 %collective-permute-start.9 = (f32[1,32,128]{2,1,0:T(8,128)S(1)}, f32[1,32,128]{2,1,0:T(8,128)S(1)}, u32[]{:S(2)}, u32[]{:S(2)}) collective-permute-start(f32[1,32,128]{2,1,0:T(8,128)S(1)} %get-tuple-element.202), channel_id=1, source_target_pairs={{32,0},{64,32},{96,64},{128,96},{160,128},{192,160},{224,192},{256... | collective-permute-start | bytes 49160 | tf_op jit(solution)/shard_map/ppermute | solution.py:39
  40.7 55.7 %all-to-all-start.1 = ((f32[32,32,128]{2,1,0:T(8,128)}), f32[32,32,128]{2,1,0:T(8,128)S(1)}, u32[]{:S(2)}, u32[]{:S(2)}) async-start(f32[32,32,128]{2,1,0:T(8,128)} %param.7), calls=%async_computation.1 | async-start | bytes 1048576 | tf_op jit(solution)/shard_map/all_to_all | solution.py:130
  53.2 4.8 %collective-permute-start.10 = (f32[34,1,128]{2,1,0:T(1,128)S(1)}, f32[34,1,128]{2,1,0:T(1,128)S(1)}, u32[]{:S(2)}, u32[]{:S(2)}) collective-permute-start(f32[34,1,128]{2,1,0:T(1,128)S(1)} %get-tuple-element.111), channel_id=1, source_target_pairs={{0,1},{1,2},{2,3},{3,4},{4,5},{5,6},{6,7},{7,8},{8,9},{9,10},{10,1... | collective-permute-start | bytes 52232 | tf_op jit(solution)/shard_map/ppermute | solution.py:38
  55.4 4.2 %collective-permute-start.11 = (f32[34,1,128]{2,1,0:T(1,128)S(1)}, f32[34,1,128]{2,1,0:T(1,128)S(1)}, u32[]{:S(2)}, u32[]{:S(2)}) collective-permute-start(f32[34,1,128]{2,1,0:T(1,128)S(1)} %get-tuple-element.112), channel_id=1, source_target_pairs={{1,0},{2,1},{3,2},{4,3},{5,4},{6,5},{7,6},{8,7},{9,8},{10,9},{11,1... | collective-permute-start | bytes 52232 | tf_op jit(solution)/shard_map/ppermute | solution.py:39
  58.0 18.7 %copy-start.2 = (f32[31,32,128]{2,1,0:T(8,128)}, f32[31,32,128]{2,1,0:T(8,128)S(1)}, u32[]{:S(2)}) copy-start(f32[31,32,128]{2,1,0:T(8,128)S(1)} %add_multiply_fusion) | copy-start | bytes 1523716
  60.6 7.1 %collective-permute-start.12 = (f32[1,32,128]{2,1,0:T(8,128)S(1)}, f32[1,32,128]{2,1,0:T(8,128)S(1)}, u32[]{:S(2)}, u32[]{:S(2)}) collective-permute-start(f32[1,32,128]{2,1,0:T(8,128)S(1)} %get-tuple-element.199), channel_id=1, source_target_pairs={{0,32},{32,64},{64,96},{96,128},{128,160},{160,192},{192,224},{224... | collective-permute-start | bytes 49160 | tf_op jit(solution)/shard_map/ppermute | solution.py:38
  63.3 6.8 %collective-permute-start.13 = (f32[1,32,128]{2,1,0:T(8,128)S(1)}, f32[1,32,128]{2,1,0:T(8,128)S(1)}, u32[]{:S(2)}, u32[]{:S(2)}) collective-permute-start(f32[1,32,128]{2,1,0:T(8,128)S(1)} %get-tuple-element.200), channel_id=1, source_target_pairs={{32,0},{64,32},{96,64},{128,96},{160,128},{192,160},{224,192},{256... | collective-permute-start | bytes 49160 | tf_op jit(solution)/shard_map/ppermute | solution.py:39
  70.1 6.5 %collective-permute-start.14 = (f32[34,1,128]{2,1,0:T(1,128)S(1)}, f32[34,1,128]{2,1,0:T(1,128)S(1)}, u32[]{:S(2)}, u32[]{:S(2)}) collective-permute-start(f32[34,1,128]{2,1,0:T(1,128)S(1)} %get-tuple-element.109), channel_id=1, source_target_pairs={{0,1},{1,2},{2,3},{3,4},{4,5},{5,6},{6,7},{7,8},{8,9},{9,10},{10,1... | collective-permute-start | bytes 52232 | tf_op jit(solution)/shard_map/ppermute | solution.py:38
  74.3 3.1 %collective-permute-start.15 = (f32[34,1,128]{2,1,0:T(1,128)S(1)}, f32[34,1,128]{2,1,0:T(1,128)S(1)}, u32[]{:S(2)}, u32[]{:S(2)}) collective-permute-start(f32[34,1,128]{2,1,0:T(1,128)S(1)} %get-tuple-element.110), channel_id=1, source_target_pairs={{1,0},{2,1},{3,2},{4,3},{5,4},{6,5},{7,6},{8,7},{9,8},{10,9},{11,1... | collective-permute-start | bytes 52232 | tf_op jit(solution)/shard_map/ppermute | solution.py:39
  78.3 7.9 %collective-permute-start.16 = (f32[1,32,128]{2,1,0:T(8,128)S(1)}, f32[1,32,128]{2,1,0:T(8,128)S(1)}, u32[]{:S(2)}, u32[]{:S(2)}) collective-permute-start(f32[1,32,128]{2,1,0:T(8,128)S(1)} %get-tuple-element.197), channel_id=1, source_target_pairs={{0,32},{32,64},{64,96},{96,128},{128,160},{160,192},{192,224},{224... | collective-permute-start | bytes 49160 | tf_op jit(solution)/shard_map/ppermute | solution.py:38
  82.0 5.8 %collective-permute-start.17 = (f32[1,32,128]{2,1,0:T(8,128)S(1)}, f32[1,32,128]{2,1,0:T(8,128)S(1)}, u32[]{:S(2)}, u32[]{:S(2)}) collective-permute-start(f32[1,32,128]{2,1,0:T(8,128)S(1)} %get-tuple-element.198), channel_id=1, source_target_pairs={{32,0},{64,32},{96,64},{128,96},{160,128},{192,160},{224,192},{256... | collective-permute-start | bytes 49160 | tf_op jit(solution)/shard_map/ppermute | solution.py:39
  87.8 5.1 %collective-permute-start.18 = (f32[34,1,128]{2,1,0:T(1,128)S(1)}, f32[34,1,128]{2,1,0:T(1,128)S(1)}, u32[]{:S(2)}, u32[]{:S(2)}) collective-permute-start(f32[34,1,128]{2,1,0:T(1,128)S(1)} %get-tuple-element.107), channel_id=1, source_target_pairs={{0,1},{1,2},{2,3},{3,4},{4,5},{5,6},{6,7},{7,8},{8,9},{9,10},{10,1... | collective-permute-start | bytes 52232 | tf_op jit(solution)/shard_map/ppermute | solution.py:38
  90.8 3.8 %collective-permute-start.19 = (f32[34,1,128]{2,1,0:T(1,128)S(1)}, f32[34,1,128]{2,1,0:T(1,128)S(1)}, u32[]{:S(2)}, u32[]{:S(2)}) collective-permute-start(f32[34,1,128]{2,1,0:T(1,128)S(1)} %get-tuple-element.108), channel_id=1, source_target_pairs={{1,0},{2,1},{3,2},{4,3},{5,4},{6,5},{7,6},{8,7},{9,8},{10,9},{11,1... | collective-permute-start | bytes 52232 | tf_op jit(solution)/shard_map/ppermute | solution.py:39
  96.4 26.3 %all-to-all-start = ((f32[32,32,128]{2,1,0:T(8,128)}), f32[32,32,128]{2,1,0:T(8,128)S(1)}, u32[]{:S(2)}, u32[]{:S(2)}) async-start(f32[32,32,128]{2,1,0:T(8,128)} %fusion.11), calls=%async_computation | async-start | bytes 1048576 | tf_op jit(solution)/shard_map/all_to_all | solution.py:129
  123.2 1.0 copy-start.7
  123.2 1.2 copy-start.8
  132.0 5.5 %copy-start.3 = (f32[31,32,128]{2,1,0:T(8,128)S(1)}, f32[31,32,128]{2,1,0:T(8,128)}, u32[]{:S(2)}) copy-start(f32[31,32,128]{2,1,0:T(8,128)} %copy-done.2) | copy-start | bytes 1523716
  133.0 15.2 %all-to-all-start.2 = ((f32[1,1024,128]{2,0,1:T(1,128)}), f32[1,1024,128]{2,0,1:T(1,128)S(1)}, u32[]{:S(2)}, u32[]{:S(2)}) async-start(f32[1,1024,128]{2,0,1:T(1,128)} %bitcast.8), calls=%async_computation.2 | async-start | bytes 1048576 | tf_op jit(solution)/shard_map/all_to_all | solution.py:111
  149.9 1.2 copy-start.10
  149.9 1.3 copy-start.11
  158.0 7.5 %collective-permute-start.20 = (f32[3,32,128]{2,1,0:T(8,128)S(1)}, f32[3,32,128]{2,1,0:T(8,128)S(1)}, u32[]{:S(2)}, u32[]{:S(2)}) collective-permute-start(f32[3,32,128]{2,1,0:T(8,128)S(1)} %pad_maximum_fusion.15), channel_id=1, source_target_pairs={{32,0},{64,32},{96,64},{128,96},{160,128},{192,160},{224,192},{256... | collective-permute-start | bytes 147464 | tf_op jit(solution)/shard_map/ppermute | solution.py:47
  166.3 7.4 %collective-permute-start.21 = (f32[1,4,32,128]{3,2,1,0:T(8,128)S(1)}, f32[1,4,32,128]{3,2,1,0:T(8,128)S(1)}, u32[]{:S(2)}, u32[]{:S(2)}) collective-permute-start(f32[1,4,32,128]{3,2,1,0:T(8,128)S(1)} %fusion.34), channel_id=1, source_target_pairs={{0,32},{32,64},{64,96},{96,128},{128,160},{160,192},{192,224},{224... | collective-permute-start | bytes 196616 | tf_op jit(solution)/shard_map/ppermute | solution.py:19
  170.2 6.2 %collective-permute-start.22 = (f32[1,4,32,128]{3,2,1,0:T(8,128)S(1)}, f32[1,4,32,128]{3,2,1,0:T(8,128)S(1)}, u32[]{:S(2)}, u32[]{:S(2)}) collective-permute-start(f32[1,4,32,128]{3,2,1,0:T(8,128)S(1)} %fusion.34), channel_id=1, source_target_pairs={{0,480},{32,0},{64,32},{96,64},{128,96},{160,128},{192,160},{224,1... | collective-permute-start | bytes 196616 | tf_op jit(solution)/shard_map/ppermute | solution.py:24
  173.7 7.4 %collective-permute-start.23 = (f32[1,4,32,128]{3,2,1,0:T(8,128)S(1)}, f32[1,4,32,128]{3,2,1,0:T(8,128)S(1)}, u32[]{:S(2)}, u32[]{:S(2)}) collective-permute-start(f32[1,4,32,128]{3,2,1,0:T(8,128)S(1)} %collective-permute-done.21), channel_id=1, source_target_pairs={{0,32},{32,64},{64,96},{96,128},{128,160},{160,192},{192,224},{224... | collective-permute-start | bytes 196616 | tf_op jit(solution)/shard_map/ppermute | solution.py:19
  176.4 6.6 %collective-permute-start.24 = (f32[1,4,32,128]{3,2,1,0:T(8,128)S(1)}, f32[1,4,32,128]{3,2,1,0:T(8,128)S(1)}, u32[]{:S(2)}, u32[]{:S(2)}) collective-permute-start(f32[1,4,32,128]{3,2,1,0:T(8,128)S(1)} %collective-permute-done.22), channel_id=1, source_target_pairs={{0,480},{32,0},{64,32},{96,64},{128,96},{160,128},{192,160},{224,1... | collective-permute-start | bytes 196616 | tf_op jit(solution)/shard_map/ppermute | solution.py:24
  181.0 7.4 %collective-permute-start.25 = (f32[1,4,32,128]{3,2,1,0:T(8,128)S(1)}, f32[1,4,32,128]{3,2,1,0:T(8,128)S(1)}, u32[]{:S(2)}, u32[]{:S(2)}) collective-permute-start(f32[1,4,32,128]{3,2,1,0:T(8,128)S(1)} %collective-permute-done.23), channel_id=1, source_target_pairs={{0,32},{32,64},{64,96},{96,128},{128,160},{160,192},{192,224},{224... | collective-permute-start | bytes 196616 | tf_op jit(solution)/shard_map/ppermute | solution.py:19
  182.9 7.4 %collective-permute-start.26 = (f32[1,4,32,128]{3,2,1,0:T(8,128)S(1)}, f32[1,4,32,128]{3,2,1,0:T(8,128)S(1)}, u32[]{:S(2)}, u32[]{:S(2)}) collective-permute-start(f32[1,4,32,128]{3,2,1,0:T(8,128)S(1)} %collective-permute-done.24), channel_id=1, source_target_pairs={{0,480},{32,0},{64,32},{96,64},{128,96},{160,128},{192,160},{224,1... | collective-permute-start | bytes 196616 | tf_op jit(solution)/shard_map/ppermute | solution.py:24
  188.4 7.4 %collective-permute-start.27 = (f32[1,4,32,128]{3,2,1,0:T(8,128)S(1)}, f32[1,4,32,128]{3,2,1,0:T(8,128)S(1)}, u32[]{:S(2)}, u32[]{:S(2)}) collective-permute-start(f32[1,4,32,128]{3,2,1,0:T(8,128)S(1)} %collective-permute-done.25), channel_id=1, source_target_pairs={{0,32},{32,64},{64,96},{96,128},{128,160},{160,192},{192,224},{224... | collective-permute-start | bytes 196616 | tf_op jit(solution)/shard_map/ppermute | solution.py:19
  190.3 7.4 %collective-permute-start.28 = (f32[1,4,32,128]{3,2,1,0:T(8,128)S(1)}, f32[1,4,32,128]{3,2,1,0:T(8,128)S(1)}, u32[]{:S(2)}, u32[]{:S(2)}) collective-permute-start(f32[1,4,32,128]{3,2,1,0:T(8,128)S(1)} %collective-permute-done.26), channel_id=1, source_target_pairs={{0,480},{32,0},{64,32},{96,64},{128,96},{160,128},{192,160},{224,1... | collective-permute-start | bytes 196616 | tf_op jit(solution)/shard_map/ppermute | solution.py:24
  195.7 7.4 %collective-permute-start.29 = (f32[1,4,32,128]{3,2,1,0:T(8,128)S(1)}, f32[1,4,32,128]{3,2,1,0:T(8,128)S(1)}, u32[]{:S(2)}, u32[]{:S(2)}) collective-permute-start(f32[1,4,32,128]{3,2,1,0:T(8,128)S(1)} %collective-permute-done.27), channel_id=1, source_target_pairs={{0,32},{32,64},{64,96},{96,128},{128,160},{160,192},{192,224},{224... | collective-permute-start | bytes 196616 | tf_op jit(solution)/shard_map/ppermute | solution.py:19
  197.7 7.4 %collective-permute-start.30 = (f32[1,4,32,128]{3,2,1,0:T(8,128)S(1)}, f32[1,4,32,128]{3,2,1,0:T(8,128)S(1)}, u32[]{:S(2)}, u32[]{:S(2)}) collective-permute-start(f32[1,4,32,128]{3,2,1,0:T(8,128)S(1)} %collective-permute-done.28), channel_id=1, source_target_pairs={{0,480},{32,0},{64,32},{96,64},{128,96},{160,128},{192,160},{224,1... | collective-permute-start | bytes 196616 | tf_op jit(solution)/shard_map/ppermute | solution.py:24
  203.1 7.4 %collective-permute-start.31 = (f32[1,4,32,128]{3,2,1,0:T(8,128)S(1)}, f32[1,4,32,128]{3,2,1,0:T(8,128)S(1)}, u32[]{:S(2)}, u32[]{:S(2)}) collective-permute-start(f32[1,4,32,128]{3,2,1,0:T(8,128)S(1)} %collective-permute-done.29), channel_id=1, source_target_pairs={{0,32},{32,64},{64,96},{96,128},{128,160},{160,192},{192,224},{224... | collective-permute-start | bytes 196616 | tf_op jit(solution)/shard_map/ppermute | solution.py:19
  205.0 7.4 %collective-permute-start.32 = (f32[1,4,32,128]{3,2,1,0:T(8,128)S(1)}, f32[1,4,32,128]{3,2,1,0:T(8,128)S(1)}, u32[]{:S(2)}, u32[]{:S(2)}) collective-permute-start(f32[1,4,32,128]{3,2,1,0:T(8,128)S(1)} %collective-permute-done.30), channel_id=1, source_target_pairs={{0,480},{32,0},{64,32},{96,64},{128,96},{160,128},{192,160},{224,1... | collective-permute-start | bytes 196616 | tf_op jit(solution)/shard_map/ppermute | solution.py:24
  210.5 7.4 %collective-permute-start.33 = (f32[1,4,32,128]{3,2,1,0:T(8,128)S(1)}, f32[1,4,32,128]{3,2,1,0:T(8,128)S(1)}, u32[]{:S(2)}, u32[]{:S(2)}) collective-permute-start(f32[1,4,32,128]{3,2,1,0:T(8,128)S(1)} %collective-permute-done.31), channel_id=1, source_target_pairs={{0,32},{32,64},{64,96},{96,128},{128,160},{160,192},{192,224},{224... | collective-permute-start | bytes 196616 | tf_op jit(solution)/shard_map/ppermute | solution.py:19
  212.4 7.4 %collective-permute-start.34 = (f32[1,4,32,128]{3,2,1,0:T(8,128)S(1)}, f32[1,4,32,128]{3,2,1,0:T(8,128)S(1)}, u32[]{:S(2)}, u32[]{:S(2)}) collective-permute-start(f32[1,4,32,128]{3,2,1,0:T(8,128)S(1)} %collective-permute-done.32), channel_id=1, source_target_pairs={{0,480},{32,0},{64,32},{96,64},{128,96},{160,128},{192,160},{224,1... | collective-permute-start | bytes 196616 | tf_op jit(solution)/shard_map/ppermute | solution.py:24
  217.8 7.4 %collective-permute-start.35 = (f32[1,4,32,128]{3,2,1,0:T(8,128)S(1)}, f32[1,4,32,128]{3,2,1,0:T(8,128)S(1)}, u32[]{:S(2)}, u32[]{:S(2)}) collective-permute-start(f32[1,4,32,128]{3,2,1,0:T(8,128)S(1)} %collective-permute-done.33), channel_id=1, source_target_pairs={{0,32},{32,64},{64,96},{96,128},{128,160},{160,192},{192,224},{224... | collective-permute-start | bytes 196616 | tf_op jit(solution)/shard_map/ppermute | solution.py:19
  (4 other events, 3.9 us)
